TPU v7x, 32 devices: a whole 2x2x4 slice. The times are simulated.
32 devices in a mesh: row: 8 (over z, x), col: 4 (over y, core).
Axes of the slice: x: 2, y: 2, z: 4, core: 2. Of those that a mesh axis runs over, the one named last changes fastest.
Arguments:
- subspace: bfloat16 [256, 32768], P('col', 'row'), may hold values from -400 to 400
- onsite: float32 [32768], P('row'), may hold values from -1.5 to 1.5
- blocks: bfloat16 [20, 256, 128, 128], P(None, 'row'), may hold values from -0.125 to 0.125
- cols: int32 [256, 20], replicated, may hold values from 0 to 255, as said below
Outputs:
- basis: float32 [256, 32768], P('col', 'row')
- factor: float32 [256, 256], replicated
Inputs may be any that keep to these rules, and one draw needn't show every extreme that they name: `cols`: the block rows are numbered by device: device r of row holds block rows r * 32 to (r + 1) * 32 - 1. A block row names block rows of its own device or of the devices r + 1, r - 1, r + 2 and r + 4 along row, counted round. The block rows of one device name between 1 and 4 distinct block rows of each of these four devices, and in every draw some device names exactly 4 on each of its four.
All inputs are finite; a program needn't handle non-finite values.
Results may differ from a plain program's by a relative error of at most 0.0044.
Values may be sent and summed in bfloat16 or wider, within the bound.
A program may use at most 128 MiB of HBM per device.

v0:
```python
import math

import jax
import jax.numpy as jnp
from jax import lax
from jax.sharding import PartitionSpec as P

S = 256
HALO = 4
FILTER = 4


filter_scale = 0.4


def pick_rows(columns, first_block, local_blocks):
    local_ids = first_block + jnp.arange(local_blocks, dtype=jnp.int32)
    hits = jnp.any(columns[..., :, None] == local_ids, axis=-2)
    ranks = jnp.cumsum(hits.astype(jnp.int32), axis=-1) - 1
    slots = jnp.arange(HALO, dtype=jnp.int32)
    select = hits[..., None, :] & (ranks[..., None, :] == slots[:, None])
    return select.astype(jnp.bfloat16)


def body(subspace, onsite, blocks, cols):
    row_count = lax.axis_size("row")
    row_index = lax.axis_index("row")
    part_width, local_rows = subspace.shape
    slot_count, local_blocks, block_size, _ = blocks.shape
    global_blocks = row_count * local_blocks
    first_block = row_index * local_blocks
    own_cols = lax.dynamic_slice_in_dim(cols, first_block, local_blocks, 0)
    every_block = jnp.arange(global_blocks, dtype=jnp.int32)
    matches = own_cols[:, :, None] == every_block
    needed = jnp.any(matches, axis=(0, 1)).astype(jnp.int32).reshape(row_count, local_blocks)
    rank_table = (jnp.cumsum(needed, axis=1) - 1).reshape(-1)
    slot_rank = jnp.sum(jnp.where(matches, rank_table, 0), axis=-1)
    owners = own_cols // local_blocks
    within = own_cols % local_blocks
    device_ids = jnp.arange(row_count, dtype=jnp.int32)
    select_all = pick_rows(
        cols.reshape(row_count, local_blocks * slot_count), first_block, local_blocks
    )
    bases = local_blocks + HALO * device_ids
    base_of = jnp.sum(jnp.where(owners[:, :, None] == device_ids, bases, 0), axis=-1)
    positions = jnp.where(owners == row_index, within, base_of + slot_rank)

    def coupled(lowered):
        shaped = lowered.reshape(part_width, local_blocks, block_size)
        outgoing = jnp.einsum(
            "dqj,cjb->cdqb", select_all, shaped, preferred_element_type=jnp.float32
        ).astype(jnp.bfloat16)
        incoming = lax.all_to_all(outgoing, "row", split_axis=1, concat_axis=1, tiled=True)
        extra = incoming.reshape(part_width, row_count * HALO, block_size)
        extended = jnp.concatenate([shaped, extra], axis=1)
        gathered = jnp.take(extended, positions, axis=1)
        product = jnp.einsum("clsa,slab->clb", gathered, blocks, preferred_element_type=jnp.float32)
        return product.reshape(part_width, local_rows) + onsite[None, :] * lowered.astype(
            jnp.float32
        )

    previous = subspace.astype(jnp.float32)
    current = filter_scale * coupled(subspace)
    for filter_step in range(FILTER - 1):
        lowered = current.astype(jnp.bfloat16)
        following = 2.0 * filter_scale * coupled(lowered) - previous
        previous, current = (current, following)
    final = current.astype(jnp.bfloat16)
    whole = lax.all_gather(final, "col", axis=0, tiled=True)
    gram_local = jnp.einsum("ar,br->ab", whole, whole, preferred_element_type=jnp.float32)
    gram = lax.psum(gram_local, "row")
    lower = jnp.linalg.cholesky(gram)
    total_rows = row_count * local_rows
    inverse = lax.linalg.triangular_solve(
        lower, jnp.eye(S, dtype=jnp.float32), left_side=True, lower=True
    )
    own_part = lax.dynamic_slice_in_dim(inverse, lax.axis_index("col") * part_width, part_width, 0)
    basis = math.sqrt(total_rows) * jnp.dot(
        own_part, whole.astype(jnp.float32), precision=lax.Precision.HIGHEST
    )
    factor = lower.T / math.sqrt(total_rows)
    return (basis, factor)


def solution(mesh):
    in_specs = (P("col", "row"), P("row"), P(None, "row", None, None), P())
    out_specs = (P("col", "row"), P())
    return jax.shard_map(body, mesh=mesh, in_specs=in_specs, out_specs=out_specs, check_vma=False)
```

profile of v0, /device:TPU:0, one launch (start us, length us, event | category | flops | bytes accessed | tf_op | source)
XLA Modules:
  0.0 388.7 jit_solution(8894773200504515112)
XLA Ops:
  7.2 0.8 copy.120
  8.1 0.3 compare_reduce_fusion
  8.5 0.2 reduce_window_sum.18
  8.6 1.1 copy.164
  9.8 0.3 fusion.44
  10.1 0.9 copy.121
  11.0 7.3 %all-to-all-start = ((bf16[64,8,4,128]{3,0,2,1:T(8,128)(2,1)}), bf16[64,8,4,128]{3,0,2,1:T(8,128)(2,1)S(1)}, u32[]{:S(2)}, u32[]{:S(2)}) async-start(bf16[64,8,4,128]{3,0,2,1:T(8,128)(2,1)} %copy.121), calls=%async_computation | async-start | bytes 1048576 | tf_op jit(solution)/shard_map/all_to_all | solution.py:53
  18.3 0.8 add_select_fusion.1
  19.1 0.2 fusion.57
  19.3 0.2 reduce_window_sum.19
  19.7 0.5 select_reduce_fusion
  20.6 1.2 copy_bitcast_fusion.3
  21.8 11.0 %all-to-all-done = bf16[64,8,4,128]{3,0,2,1:T(8,128)(2,1)S(1)} async-done(((bf16[64,8,4,128]{3,0,2,1:T(8,128)(2,1)}), bf16[64,8,4,128]{3,0,2,1:T(8,128)(2,1)S(1)}, u32[]{:S(2)}, u32[]{:S(2)}) %all-to-all-start) | async-done | bytes 524320 | tf_op jit(solution)/shard_map/all_to_all | solution.py:53
  32.9 18.0 %gather_fusion = bf16[640,64,128]{2,1,0:T(8,128)(2,1)} fusion(bf16[64,64,128]{2,0,1:T(8,128)(2,1)S(1)} %pad_maximum_fusion, s32[1024]{0:T(1024)S(1)} %pad_clamp_fusion), kind=kCustom, calls=%fused_computation.clone | custom fusion | bytes 20974080 | tf_op jit(solution)/shard_map/jit(_take)/gather | solution.py:56
  50.9 12.4 %fusion.24 = f32[32,8,8,128]{3,2,1,0:T(8,128)S(1)} fusion(bf16[20,32,128,128]{3,2,1,0:T(8,128)(2,1)} %param.8, bf16[32,20,64,128]{3,2,1,0:T(8,128)(2,1)} %bitcast.185, pred[32,20]{1,0:T(8,128)(4,1)S(1)} %copy.116), kind=kOutput, calls=%fused_computation.31 | convolution fusion | flops 1347420160 | bytes 32506496 | tf_op jit(solution)/shard_map/clsa,slab->clb/dot_general | solution.py:57
  63.6 0.3 fusion.45
  63.9 1.0 copy.126
  64.9 3.9 all-to-all-start.1
  68.9 14.5 %all-to-all-done.1 = bf16[64,8,4,128]{3,2,0,1:T(4,128)(2,1)S(1)} async-done(((bf16[64,8,4,128]{3,2,0,1:T(4,128)(2,1)}), bf16[64,8,4,128]{3,2,0,1:T(4,128)(2,1)S(1)}, u32[]{:S(2)}, u32[]{:S(2)}) %all-to-all-start.1) | async-done | bytes 524320 | tf_op jit(solution)/shard_map/all_to_all | solution.py:53
  83.7 18.0 %gather_fusion.1 = bf16[640,64,128]{2,1,0:T(8,128)(2,1)} fusion(bf16[64,64,128]{2,0,1:T(8,128)(2,1)S(1)} %pad_maximum_fusion.1, s32[1024]{0:T(1024)S(1)} %pad_clamp_fusion), kind=kCustom, calls=%fused_computation.1.clone | custom fusion | bytes 20974080 | tf_op jit(solution)/shard_map/jit(_take)/gather | solution.py:56
  101.7 12.4 %fusion.29 = f32[32,8,8,128]{3,2,1,0:T(8,128)S(1)} fusion(bf16[20,32,128,128]{3,2,1,0:T(8,128)(2,1)} %param.8, bf16[32,20,64,128]{3,2,1,0:T(8,128)(2,1)} %bitcast.186, pred[32,20]{1,0:T(8,128)(4,1)S(1)} %copy.116), kind=kOutput, calls=%fused_computation.32 | convolution fusion | flops 1347420160 | bytes 32506496 | tf_op jit(solution)/shard_map/clsa,slab->clb/dot_general | solution.py:57
  114.1 0.2 fusion.64
  114.4 0.3 fusion.46
  114.7 1.0 copy.132
  115.7 3.9 %all-to-all-start.2 = ((bf16[64,8,4,128]{3,2,0,1:T(4,128)(2,1)}), bf16[64,8,4,128]{3,2,0,1:T(4,128)(2,1)S(1)}, u32[]{:S(2)}, u32[]{:S(2)}) async-start(bf16[64,8,4,128]{3,2,0,1:T(4,128)(2,1)} %copy.132), calls=%async_computation.2 | async-start | bytes 1048576 | tf_op jit(solution)/shard_map/all_to_all | solution.py:53
  119.7 1.0 copy_bitcast_fusion.1
  120.6 13.7 %all-to-all-done.2 = bf16[64,8,4,128]{3,2,0,1:T(4,128)(2,1)S(1)} async-done(((bf16[64,8,4,128]{3,2,0,1:T(4,128)(2,1)}), bf16[64,8,4,128]{3,2,0,1:T(4,128)(2,1)S(1)}, u32[]{:S(2)}, u32[]{:S(2)}) %all-to-all-start.2) | async-done | bytes 524320 | tf_op jit(solution)/shard_map/all_to_all | solution.py:53
  134.4 1.1 pad_maximum_fusion.2
  135.6 18.0 %gather_fusion.2 = bf16[640,64,128]{2,1,0:T(8,128)(2,1)} fusion(bf16[64,64,128]{2,0,1:T(8,128)(2,1)S(1)} %pad_maximum_fusion.2, s32[1024]{0:T(1024)S(1)} %pad_clamp_fusion), kind=kCustom, calls=%fused_computation.2.clone | custom fusion | bytes 20974080 | tf_op jit(solution)/shard_map/jit(_take)/gather | solution.py:56
  153.6 12.4 %fusion.34 = f32[32,8,8,128]{3,2,1,0:T(8,128)S(1)} fusion(bf16[20,32,128,128]{3,2,1,0:T(8,128)(2,1)} %param.8, bf16[32,20,64,128]{3,2,1,0:T(8,128)(2,1)} %bitcast.187, pred[32,20]{1,0:T(8,128)(4,1)S(1)} %copy.116), kind=kOutput, calls=%fused_computation.33 | convolution fusion | flops 1347420160 | bytes 32506496 | tf_op jit(solution)/shard_map/clsa,slab->clb/dot_general | solution.py:57
  166.0 0.4 fusion.55
  166.5 0.3 fusion.47
  166.8 1.0 copy.138
  167.8 3.7 all-to-all-start.3
  171.4 0.5 all-gather.2.cloned.1.call-start
  171.9 0.9 copy_bitcast_fusion
  172.9 13.2 %all-to-all-done.3 = bf16[64,8,4,128]{3,2,0,1:T(4,128)(2,1)S(1)} async-done(((bf16[64,8,4,128]{3,2,0,1:T(4,128)(2,1)}), bf16[64,8,4,128]{3,2,0,1:T(4,128)(2,1)S(1)}, u32[]{:S(2)}, u32[]{:S(2)}) %all-to-all-start.3) | async-done | bytes 524320 | tf_op jit(solution)/shard_map/all_to_all | solution.py:53
  186.2 1.1 pad_maximum_fusion.3
  187.4 18.0 %gather_fusion.3 = bf16[640,64,128]{2,1,0:T(8,128)(2,1)} fusion(bf16[64,64,128]{2,0,1:T(8,128)(2,1)S(1)} %pad_maximum_fusion.3, s32[1024]{0:T(1024)S(1)} %pad_clamp_fusion), kind=kCustom, calls=%fused_computation.3.clone | custom fusion | bytes 20974080 | tf_op jit(solution)/shard_map/jit(_take)/gather | solution.py:56
  205.4 12.4 %fusion.39 = f32[32,8,8,128]{3,2,1,0:T(8,128)S(1)} fusion(bf16[20,32,128,128]{3,2,1,0:T(8,128)(2,1)} %param.8, bf16[32,20,64,128]{3,2,1,0:T(8,128)(2,1)} %bitcast.184, pred[32,20]{1,0:T(8,128)(4,1)S(1)} %copy.116), kind=kOutput, calls=%fused_computation.34 | convolution fusion | flops 1347420160 | bytes 32506496 | tf_op jit(solution)/shard_map/clsa,slab->clb/dot_general | solution.py:57
  217.8 1.2 fusion.52
  219.1 0.2 all-reduce.3.cloned.1.call-start
  219.3 21.6 %all-gather.2.cloned.1.call-done = bf16[256,4096]{1,0:T(8,128)(2,1)} async-done(((bf16[64,4096]{1,0:T(8,128)(2,1)}), bf16[256,4096]{1,0:T(8,128)(2,1)}) %all-gather.2.cloned.1.call-update) | async-done | bytes 2097168 | tf_op jit(solution)/shard_map/all_gather | solution.py:69
  240.9 3.8 fusion.99
  244.8 71.1 %all-reduce.3.cloned.1.call-done = f32[256,256]{0,1:T(8,128)} async-done(((f32[256,256]{0,1:T(8,128)}), f32[256,256]{0,1:T(8,128)}) %all-reduce.3.cloned.1.call-update) | async-done | bytes 262160 | tf_op jit(solution)/shard_map/psum | solution.py:71
  315.9 1.1 copy.145
  317.0 1.0 fusion.62
  318.0 11.7 %cholesky.50 = f32[128,128]{1,0:T(8,128)S(1)} custom-call(f32[128,128]{1,0:T(8,128)S(1)} %cholesky.118), custom_call_target="Cholesky" | custom-call | tf_op jit(solution)/shard_map/jit(cholesky)/cholesky | solution.py:72
  329.8 9.8 %custom-call.14 = f32[1,128,128]{1,2,0:T(8,128)S(1)} custom-call(f32[1,128,128]{2,1,0:T(8,128)S(1)} %get-tuple-element.40), custom_call_target="InvertDiagBlocksLowerTriangular" | custom-call | tf_op jit(solution)/shard_map/jit(cholesky)/cholesky | solution.py:72
  339.6 0.2 constant_dynamic-update-slice_fusion
  339.8 0.3 convolution_subtract_fusion.1
  340.0 11.7 %cholesky.105 = f32[128,128]{1,0:T(8,128)S(1)} custom-call(f32[128,128]{1,0:T(8,128)S(1)} %convolution_subtract_fusion.1), custom_call_target="Cholesky" | custom-call | tf_op jit(solution)/shard_map/jit(cholesky)/cholesky | solution.py:72
  351.8 0.6 compare_reduce_fusion.1
  353.9 4.2 %while.1 = (s32[]{:T(128)}, f32[256,256]{1,0:T(8,128)S(1)}, s32[2,2]{1,0:T(2,128)S(1)}, f32[2,128,128]{2,1,0:T(8,128)S(1)}, s32[]{:T(128)}) while((s32[]{:T(128)}, f32[256,256]{1,0:T(8,128)S(1)}, s32[2,2]{1,0:T(2,128)S(1)}, f32[2,128,128]{2,1,0:T(8,128)S(1)}, s32[]{:T(128)}) %tuple.36), condition=%wide.while_cond, body=%wide.while_body.sunk | while | flops 2 | bytes 131181 | solution.py:74
  354.1 0.6 fusion.113
  354.7 1.4 bitcast_dynamic-update-slice_fusion.2
  356.1 0.6 fusion.113
  356.7 1.4 bitcast_dynamic-update-slice_fusion.2
  358.1 19.7 %custom-call.15 = f32[2,128,128]{1,2,0:T(8,128)S(1)} custom-call(f32[2,128,128]{2,1,0:T(8,128)S(1)} %get-tuple-element.10), custom_call_target="InvertDiagBlocksLowerTriangular" | custom-call | tf_op jit(solution)/shard_map/triangular_solve | solution.py:74
  377.7 0.3 fusion.65
  378.0 0.3 convolution_subtract_fusion
  378.3 0.3 fusion.70
  378.6 0.8 copy.146
  379.4 2.2 convolution_multiply_fusion
  (52 shorter events, 2.2 us)
Async XLA Ops:
  11.0 21.8 %all-to-all-start = ((bf16[64,8,4,128]{3,0,2,1:T(8,128)(2,1)}), bf16[64,8,4,128]{3,0,2,1:T(8,128)(2,1)S(1)}, u32[]{:S(2)}, u32[]{:S(2)}) async-start(bf16[64,8,4,128]{3,0,2,1:T(8,128)(2,1)} %copy.121), calls=%async_computation | async-start | bytes 1048576 | tf_op jit(solution)/shard_map/all_to_all | solution.py:53
  50.9 12.4 %copy-start.1 = (bf16[64,4096]{1,0:T(8,128)(2,1)S(1)}, bf16[64,4096]{1,0:T(8,128)(2,1)}, u32[]{:S(2)}) copy-start(bf16[64,4096]{1,0:T(8,128)(2,1)} %param.6) | copy-start | bytes 1572868
  50.9 12.4 %copy-start.6 = (f32[4096]{0:T(1024)S(1)}, f32[4096]{0:T(1024)}, u32[]{:S(2)}) copy-start(f32[4096]{0:T(1024)} %param.7) | copy-start | bytes 49156
  63.3 20.2 %copy-start.2 = (f32[32,8,8,128]{3,2,1,0:T(8,128)}, f32[32,8,8,128]{3,2,1,0:T(8,128)S(1)}, u32[]{:S(2)}) copy-start(f32[32,8,8,128]{3,2,1,0:T(8,128)S(1)} %fusion.24) | copy-start | bytes 3145732
  64.9 18.5 %all-to-all-start.1 = ((bf16[64,8,4,128]{3,2,0,1:T(4,128)(2,1)}), bf16[64,8,4,128]{3,2,0,1:T(4,128)(2,1)S(1)}, u32[]{:S(2)}, u32[]{:S(2)}) async-start(bf16[64,8,4,128]{3,2,0,1:T(4,128)(2,1)} %copy.126), calls=%async_computation.1 | async-start | bytes 1048576 | tf_op jit(solution)/shard_map/all_to_all | solution.py:53
  114.1 20.3 %copy-start.4 = (f32[32,8,8,128]{3,2,1,0:T(8,128)}, f32[32,8,8,128]{3,2,1,0:T(8,128)S(1)}, u32[]{:S(2)}) copy-start(f32[32,8,8,128]{3,2,1,0:T(8,128)S(1)} %fusion.29) | copy-start | bytes 3145732
  115.7 18.6 %all-to-all-start.2 = ((bf16[64,8,4,128]{3,2,0,1:T(4,128)(2,1)}), bf16[64,8,4,128]{3,2,0,1:T(4,128)(2,1)S(1)}, u32[]{:S(2)}, u32[]{:S(2)}) async-start(bf16[64,8,4,128]{3,2,0,1:T(4,128)(2,1)} %copy.132), calls=%async_computation.2 | async-start | bytes 1048576 | tf_op jit(solution)/shard_map/all_to_all | solution.py:53
  153.6 12.5 %copy-start.3 = (f32[32,8,8,128]{3,2,1,0:T(8,128)S(1)}, f32[32,8,8,128]{3,2,1,0:T(8,128)}, u32[]{:S(2)}) copy-start(f32[32,8,8,128]{3,2,1,0:T(8,128)} %copy-done.2) | copy-start | bytes 3145732
  167.8 18.3 %all-to-all-start.3 = ((bf16[64,8,4,128]{3,2,0,1:T(4,128)(2,1)}), bf16[64,8,4,128]{3,2,0,1:T(4,128)(2,1)S(1)}, u32[]{:S(2)}, u32[]{:S(2)}) async-start(bf16[64,8,4,128]{3,2,0,1:T(4,128)(2,1)} %copy.138), calls=%async_computation.3 | async-start | bytes 1048576 | tf_op jit(solution)/shard_map/all_to_all | solution.py:53
  171.4 69.4 %all-gather.2.cloned.1.call-start = ((), (), s32[]{:S(2)}) async-start(), calls=%async_computation.4 | async-start | bytes 2621440 | tf_op jit(solution)/shard_map/all_gather | solution.py:69
  205.4 12.4 %copy-start.5 = (f32[32,8,8,128]{3,2,1,0:T(8,128)S(1)}, f32[32,8,8,128]{3,2,1,0:T(8,128)}, u32[]{:S(2)}) copy-start(f32[32,8,8,128]{3,2,1,0:T(8,128)} %copy-done.4) | copy-start | bytes 3145732
  219.1 96.8 %all-reduce.3.cloned.1.call-start = ((), (), s32[]{:S(2)}) async-start(), calls=%async_computation.5 | async-start | bytes 524288 | tf_op jit(solution)/shard_map/psum | solution.py:71
  240.9 138.6 %copy-start = (bf16[256,4096]{1,0:T(8,128)(2,1)S(1)}, bf16[256,4096]{1,0:T(8,128)(2,1)}, u32[]{:S(2)}) copy-start(bf16[256,4096]{1,0:T(8,128)(2,1)} %all-gather.2.cloned.1.call-done) | copy-start | bytes 6291460
Sparse Core Ops, SparseCore 0:
  219.2 21.6 all-gather.1
  244.8 70.9 all-reduce.2
where the time goes:
time: 397 us; the launch traced here: 389 us
  waiting for transfers between devices  145 us (37%)
  local copies, waits for them, and re-layouts  88.3 us (22%)
  other arithmetic  61.4 us (15%)
  matrix products  58.1 us (15%)
  starting transfers between devices  19.5 us (5%)
  between operations  16 us (4%)
    gather x4, local copies, waits for them, and re-layouts, coupled(): gathered = jnp.take(extended, positions, axis=1)  72.1 us
    psum x1, waiting for transfers between devices, body(): gram = lax.psum(gram_local, 'row')  71.1 us
    all_to_all x4, waiting for transfers between devices, coupled(): lax.all_to_all(outgoing, 'row', split_axis=1, concat_axis=1, tiled=True)  52.4 us
    dot_general x4, matrix products, coupled(): jnp.einsum('clsa,slab->clb', gathered, blocks, preferred_element_type=jnp...  49.6 us
    another operation x6, other arithmetic, body(): lower = jnp.linalg.cholesky(gram)  33.9 us
    all_gather x1, waiting for transfers between devices, body(): whole = lax.all_gather(final, 'col', axis=0, tiled=True)  21.6 us
    another operation x2, other arithmetic, body(): lax.linalg.triangular_solve(lower, jnp.eye(S, dtype=jnp.float32), left_si...  19.7 us
    all_to_all x4, starting transfers between devices, coupled(): lax.all_to_all(outgoing, 'row', split_axis=1, concat_axis=1, tiled=True)  18.8 us
  transfers between devices with their start and end apart: 6, of which 6 were waited for; matrix products, arithmetic and copies ran while one was open for 1% of the time, Pallas kernels for 0%

commit v1 on v0

v1 whole, which is shorter than its diff:
```python
import math

import jax
import jax.numpy as jnp
from jax import lax
from jax.experimental import pallas as pl
from jax.experimental.pallas import tpu as pltpu
from jax.sharding import PartitionSpec as P

HALO = 4
FILTER = 4
UNROLL = 4
filter_scale = 0.4
f32 = jnp.float32
bf16 = jnp.bfloat16


def shifts_of(rows):
    return (rows // 2, 2, 1, -1)


def index_tables(cols, rows, me, lb):
    sc = cols.shape[1]
    shifts = shifts_of(rows)
    groups = len(shifts)
    own = lax.dynamic_slice_in_dim(cols, me * lb, lb, 0).reshape(-1)
    askers = [
        lax.dynamic_slice_in_dim(cols, lax.rem(me - d + rows, rows) * lb, lb, 0).reshape(-1)
        for d in shifts
    ]
    owners = jnp.stack([lax.rem(me + d + rows, rows) for d in shifts])
    k = jnp.arange(lb, dtype=jnp.int32)
    wanted = own[None, :] - owners[:, None] * lb
    asked = jnp.stack(askers) - me * lb
    rel = jnp.concatenate([wanted, asked], 0)
    hit = jnp.any(rel[:, :, None] == k, axis=1)
    before = (k[:, None] < k[None, :])
    rank = jnp.sum((hit[:, :, None] & before[None]).astype(jnp.int32), axis=1)
    hit_e, rank_e = hit[groups:], rank[groups:]
    g = jnp.arange(groups, dtype=jnp.int32)
    key = jnp.min(jnp.where(hit_e, g[:, None], groups), axis=0)
    ahead = (key[:, None] < key[None, :]) | ((key[:, None] == key[None, :]) & before)
    inv = jnp.sum(ahead.astype(jnp.int32), axis=0)
    perm = jnp.sum(jnp.where(inv[None, :] == k[:, None], k[None, :], 0), axis=1)
    m = jnp.arange(HALO, dtype=jnp.int32)
    pick = hit_e[:, None, :] & (rank_e[:, None, :] == m[:, None])
    exp_n = jnp.sum(jnp.where(pick, k, 0), axis=-1)
    exp_p = jnp.sum(jnp.where(pick, inv, 0), axis=-1)
    slot = lb + HALO * g[:, None] + rank[:groups]
    match = wanted[:, :, None] == k
    far = jnp.sum(jnp.where(match, slot[:, None, :], 0), axis=(0, 2))
    near = own - me * lb
    mine = (near >= 0) & (near < lb)
    near_p = jnp.sum(jnp.where(near[:, None] == k, inv, 0), axis=1)
    pos_n = jnp.where(mine, near, far)
    pos_p = jnp.where(mine, near_p, far)
    return jnp.concatenate(
        [pos_n, pos_p, perm, inv, exp_n.reshape(-1), exp_p.reshape(-1)]
    ).astype(jnp.int32)


def filter_kernel(rows, lb, sc, tab, sub, ons, blk, out, bm, x0, x1, x2, x3, s0, y1, y2, y3,
                  snd0, snd1, snd2, snd3, bsem, xsem, csem, ssem, rsem):
    me = lax.axis_index("row")
    shifts = shifts_of(rows)
    groups = len(shifts)
    pn, pp = 0, lb * sc
    pperm = 2 * lb * sc
    pinv = pperm + lb
    pexn = pinv + lb
    pexp = pexn + groups * HALO
    xs, snds = (x0, x1, x2, x3), (snd0, snd1, snd2, snd3)
    bs = blk.shape[-1]
    chunks = lb // UNROLL

    def load(c):
        part = pl.ds(c * UNROLL, UNROLL)
        return pltpu.make_async_copy(blk.at[:, part], bm.at[:, part], bsem.at[c])

    def first(i):
        cut = pl.ds(pl.multiple_of(i * bs, bs), bs)
        return (pltpu.make_async_copy(sub.at[:, cut], x0.at[i], xsem.at[i]),
                pltpu.make_async_copy(sub.at[:, cut], s0.at[i], csem.at[i]))

    @pl.loop(0, lb)
    def _(i):
        a, b = first(i)
        b.start()
        a.start()

    @pl.loop(0, chunks)
    def _(c):
        load(c).start()

    barrier = pltpu.get_barrier_semaphore()
    for d in shifts:
        pl.semaphore_signal(barrier, inc=1, device_id={"row": lax.rem(me + d + rows, rows)},
                            device_id_type=pl.DeviceIdType.MESH)

    def copy(k, g):
        return pltpu.make_async_remote_copy(
            src_ref=snds[k].at[pl.ds(g * HALO, HALO)],
            dst_ref=xs[k].at[pl.ds(lb + g * HALO, HALO)],
            send_sem=ssem.at[k, g], recv_sem=rsem.at[k, g],
            device_id={"row": lax.rem(me - shifts[g] + rows, rows)},
            device_id_type=pl.DeviceIdType.MESH)

    def pack(k, g, source, base):
        for m in range(HALO):
            snds[k][g * HALO + m] = source[tab[base + g * HALO + m]].astype(bf16)

    @pl.loop(0, lb)
    def _(i):
        first(i)[1].wait()

    for g in range(groups):
        pack(0, g, s0, pexn)
    pl.semaphore_wait(barrier, groups)

    @pl.loop(0, lb)
    def _(i):
        first(i)[0].wait()

    for g in range(groups):
        copy(0, g).start()

    def product(k, j):
        i = tab[pperm + j] if k in (1, 2) else j
        own = {0: j, 1: i, 2: j, 3: tab[pinv + j]}[k]
        base = pn if k < 2 else pp
        x = xs[k]
        left = jnp.concatenate([x[tab[base + i * sc + s]] for s in range(sc)], axis=1)
        right = jnp.concatenate([bm[s, i] for s in range(sc)], axis=0)
        acc = jnp.dot(left, right, preferred_element_type=f32)
        total = acc + ons[i] * x[own].astype(f32)
        if k == 0:
            return filter_scale * total
        prev = x0[i].astype(f32) if k == 1 else (y1[i] if k == 2 else y2[own])
        return 2.0 * filter_scale * total - prev

    for k in range(FILTER):
        for g in range(groups):
            copy(k, g).wait_recv()
        ys = (y1, y2, y3, None)[k]

        @pl.loop(0, chunks)
        def _(c):
            if k == 0:
                load(c).wait()
            if k in (1, 2):
                for g in range(groups):
                    @pl.when(c == g + 1)
                    def _():
                        pack(k + 1, g, ys, pexp)
            for u in range(UNROLL):
                j = c * UNROLL + u
                value = product(k, j)
                low = value.astype(bf16)
                if k < FILTER - 1:
                    xs[k + 1][j] = low
                    ys[j] = value
                else:
                    out[j] = low
                if k in (1, 2) and u == 1:
                    for g in range(groups):
                        @pl.when(c == g + 1)
                        def _():
                            copy(k + 1, g).start()

        if k == 0:
            for g in range(groups):
                pack(1, g, ys, pexn)
            for g in range(groups):
                copy(1, g).start()

    for k in range(FILTER):
        for g in range(groups):
            copy(k, g).wait_send()


def filtered(subspace, onsite, blocks, cols):
    rows = lax.axis_size("row")
    me = lax.axis_index("row")
    width = subspace.shape[0]
    sc, lb, bs, _ = blocks.shape
    groups = len(shifts_of(rows))
    tab = index_tables(cols, rows, me, lb)
    ext = lb + groups * HALO
    vm, dma = pltpu.VMEM, pltpu.SemaphoreType.DMA
    import functools
    return pl.pallas_call(
        functools.partial(filter_kernel, rows, lb, sc),
        out_shape=jax.ShapeDtypeStruct((lb, width, bs), bf16),
        in_specs=[pl.BlockSpec(memory_space=pltpu.SMEM), pl.BlockSpec(memory_space=pl.ANY),
                  pl.BlockSpec(memory_space=pltpu.VMEM), pl.BlockSpec(memory_space=pl.ANY)],
        out_specs=pl.BlockSpec(memory_space=pltpu.VMEM),
        scratch_shapes=[vm((sc, lb, bs, bs), bf16)]
        + [vm((ext, width, bs), bf16)] * 4
        + [vm((lb, width, bs), bf16)]
        + [vm((lb, width, bs), f32)] * 3
        + [vm((groups * HALO, width, bs), bf16)] * 4
        + [dma((lb // UNROLL,)), dma((lb,)), dma((lb,)), dma((FILTER, groups)), dma((FILTER, groups))],
        compiler_params=pltpu.CompilerParams(
            collective_id=0, has_side_effects=True, vmem_limit_bytes=56 * 1024 * 1024),
        name="filter",
    )(tab, subspace, onsite.reshape(lb, 1, bs), blocks)


def body(subspace, onsite, blocks, cols):
    row_count = lax.axis_size("row")
    part_width, local_rows = subspace.shape
    final = filtered(subspace, onsite, blocks, cols)
    final = jnp.transpose(final, (1, 0, 2)).reshape(part_width, local_rows)
    S = part_width * lax.axis_size("col")
    whole = lax.all_gather(final, "col", axis=0, tiled=True)
    gram_local = jnp.einsum("ar,br->ab", whole, whole, preferred_element_type=jnp.float32)
    gram = lax.psum(gram_local, "row")
    lower = jnp.linalg.cholesky(gram)
    total_rows = row_count * local_rows
    inverse = lax.linalg.triangular_solve(
        lower, jnp.eye(S, dtype=jnp.float32), left_side=True, lower=True
    )
    own_part = lax.dynamic_slice_in_dim(inverse, lax.axis_index("col") * part_width, part_width, 0)
    basis = math.sqrt(total_rows) * jnp.dot(
        own_part, whole.astype(jnp.float32), precision=lax.Precision.HIGHEST
    )
    factor = lower.T / math.sqrt(total_rows)
    return (basis, factor)


def solution(mesh):
    in_specs = (P("col", "row"), P("row"), P(None, "row", None, None), P())
    out_specs = (P("col", "row"), P())
    return jax.shard_map(body, mesh=mesh, in_specs=in_specs, out_specs=out_specs, check_vma=False)
```

time: 397 us -> 231 us (0.58); the launches traced: 389 us -> 230 us
  local copies, waits for them, and re-layouts: 88.3 us -> 10.5 us
  waiting for transfers between devices: 145 us -> 91.9 us
  matrix products: 58.1 us -> 7.17 us
  Pallas kernels: 0 us -> 48.1 us
  starting transfers between devices: 19.5 us -> 0.26 us
  other arithmetic: 61.4 us -> 56.6 us
    gather x4 -> x0, local copies, waits for them, and re-layouts: 72.1 us -> none  [coupled(): gathered = jnp.take(extended, positions, axis=1)]
    all_to_all x4 -> x0, waiting for transfers between devices: 52.4 us -> none  [coupled(): lax.all_to_all(outgoing, 'row', split_axis=1, concat_axis=1, tiled=True)]
    dot_general x8 -> x0, matrix products: 50.7 us -> none  [the longest x4 49.6 us: coupled(): jnp.einsum('clsa,slab->clb', gathered, blocks, preferred_element_type=jnp...]
    pallas_call x0 -> x1, Pallas kernels: none -> 48.1 us  [filtered(): pl.pallas_call(functools.partial(filter_kernel, rows, lb, sc), out_shape=...]
    all_to_all x4 -> x0, starting transfers between devices: 18.8 us -> none  [coupled(): lax.all_to_all(outgoing, 'row', split_axis=1, concat_axis=1, tiled=True)]
    convert_element_type x5 -> x0, local copies, waits for them, and re-layouts: 3.98 us -> none  [the longest x4 3.9 us: coupled(): outgoing = jnp.einsum('dqj,cjb->cdqb', select_all, shaped, preferred_elem...]
    another operation x6 -> x7, other arithmetic: 33.9 us -> 34.6 us  [body(): lower = jnp.linalg.cholesky(gram)]
  transfers between devices with their start and end apart: 6 -> 2, of which waited for: 6 -> 2; matrix products, arithmetic and copies ran while one was open for 1% -> 0% of each run, Pallas kernels for 0% -> 0%
where the time goes in v1:
time: 231 us; the launch traced here: 230 us
  waiting for transfers between devices  91.9 us (40%)
  other arithmetic  56.6 us (25%)
  Pallas kernels  48.1 us (21%)
  between operations  15.6 us (7%)
  local copies, waits for them, and re-layouts  10.5 us (5%)
  matrix products  7.17 us (3%)
    psum x1, waiting for transfers between devices, body(): gram = lax.psum(gram_local, 'row')  71.2 us
    pallas_call x1, Pallas kernels, filtered(): pl.pallas_call(functools.partial(filter_kernel, rows, lb, sc), out_shape=...  48.1 us
    another operation x7, other arithmetic, body(): lower = jnp.linalg.cholesky(gram)  34.6 us
    all_gather x1, waiting for transfers between devices, body(): whole = lax.all_gather(final, 'col', axis=0, tiled=True)  20.7 us
    another operation x2, other arithmetic, body(): lax.linalg.triangular_solve(lower, jnp.eye(S, dtype=jnp.float32), left_si...  19.7 us
  transfers between devices with their start and end apart: 2, of which 2 were waited for; matrix products, arithmetic and copies ran while one was open for 0% of the time, Pallas kernels for 0%

profile of v1, /device:TPU:0, one launch (start us, length us, event | category | flops | bytes accessed | tf_op | source)
XLA Modules:
  0.0 230.2 jit_solution(9059134795506725641)
XLA Ops:
  7.2 0.0 all-gather.2.cloned.1.call-start
  7.3 0.9 constant_dynamic-slice_fusion.5
  8.2 0.1 copy.18
  8.3 0.1 reshape.131
  8.4 0.1 copy.20
  8.5 0.1 stack_reshape.13
  8.6 0.1 copy.19
  8.7 0.1 stack_reshape.12
  8.8 0.1 copy.22
  8.9 0.1 stack_reshape.15
  9.0 0.1 copy.21
  9.1 0.1 stack_reshape.14
  9.2 0.1 add_multiply_fusion
  9.3 0.1 add_subtract_fusion
  9.4 0.2 fusion
  9.6 0.1 convert_reduce_fusion
  9.7 0.1 fusion.18
  9.8 0.1 select_reduce_fusion
  9.9 0.1 convert_reduce_fusion.1
  10.0 0.1 select_reduce_fusion.4
  10.1 0.2 select_reduce_fusion.5
  10.4 0.1 reshape.133
  10.4 0.1 reshape.132
  10.5 0.1 select_reduce_fusion.1
  10.6 0.7 concatenate.13.tab
  11.3 48.1 %filter.1 = bf16[32,64,128]{2,1,0:T(8,128)(2,1)} custom-call(s32[1376]{0:T(1024)} %concatenate.13.tab, bf16[64,4096]{1,0:T(8,128)(2,1)} %sub.54, f32[32,1,128]{2,1,0:T(1,128)} %bitcast.47, bf16[20,32,128,128]{3,2,1,0:T(8,128)(2,1)} %blk.1), custom_call_target="tpu_custom_call" | custom-call | tf_op jit(solution)/shard_map/filter/pallas_call | solution.py:191
  59.4 1.9 copy_bitcast_fusion
  61.3 0.0 all-gather.2.cloned.1.call-update
  61.3 0.2 all-reduce.3.cloned.1.call-start
  61.5 20.7 %all-gather.2.cloned.1.call-done = bf16[256,4096]{1,0:T(8,128)(2,1)} async-done(((bf16[64,4096]{1,0:T(8,128)(2,1)}), bf16[256,4096]{1,0:T(8,128)(2,1)}) %all-gather.2.cloned.1.call-update) | async-done | bytes 2097168 | tf_op jit(solution)/shard_map/all_gather | solution.py:215
  82.2 3.7 %fusion.19 = f32[256,256]{0,1:T(8,128)} fusion(bf16[256,4096]{1,0:T(8,128)(2,1)} %all-gather.2.cloned.1.call-done), kind=kOutput, calls=%fused_computation.70 | convolution fusion | flops 536870912 | bytes 2359296 | tf_op jit(solution)/shard_map/ar,br->ab/dot_general | solution.py:216
  85.9 0.0 all-reduce.3.cloned.1.call-update
  86.0 71.2 %all-reduce.3.cloned.1.call-done = f32[256,256]{0,1:T(8,128)} async-done(((f32[256,256]{0,1:T(8,128)}), f32[256,256]{0,1:T(8,128)}) %all-reduce.3.cloned.1.call-update) | async-done | bytes 262160 | tf_op jit(solution)/shard_map/psum | solution.py:217
  157.2 1.1 copy.25
  158.3 1.0 fusion.1
  159.3 11.7 %cholesky.50 = f32[128,128]{1,0:T(8,128)S(1)} custom-call(f32[128,128]{1,0:T(8,128)S(1)} %cholesky.118), custom_call_target="Cholesky" | custom-call | tf_op jit(solution)/shard_map/jit(cholesky)/cholesky | solution.py:218
  171.0 0.0 copy-start
  171.1 0.6 compare_reduce_fusion.1
  171.7 9.8 %custom-call.14 = f32[1,128,128]{1,2,0:T(8,128)S(1)} custom-call(f32[1,128,128]{2,1,0:T(8,128)S(1)} %get-tuple-element.35), custom_call_target="InvertDiagBlocksLowerTriangular" | custom-call | tf_op jit(solution)/shard_map/jit(cholesky)/cholesky | solution.py:218
  181.5 0.2 constant_dynamic-update-slice_fusion
  181.7 0.3 convolution_subtract_fusion.1
  182.0 11.7 %cholesky.105 = f32[128,128]{1,0:T(8,128)S(1)} custom-call(f32[128,128]{1,0:T(8,128)S(1)} %convolution_subtract_fusion.1), custom_call_target="Cholesky" | custom-call | tf_op jit(solution)/shard_map/jit(cholesky)/cholesky | solution.py:218
  193.8 0.6 compare_reduce_fusion
  195.8 0.8 copy.26
  196.6 0.1 triangular_solve.63
  196.7 3.9 %while.1 = (s32[]{:T(128)}, f32[256,256]{1,0:T(8,128)S(1)}, s32[2,2]{1,0:T(2,128)S(1)}, f32[2,128,128]{2,1,0:T(8,128)S(1)}, s32[]{:T(128)}) while((s32[]{:T(128)}, f32[256,256]{1,0:T(8,128)S(1)}, s32[2,2]{1,0:T(2,128)S(1)}, f32[2,128,128]{2,1,0:T(8,128)S(1)}, s32[]{:T(128)}) %tuple.38), condition=%wide.while_cond, body=%wide.while_body.sunk | while | flops 2 | bytes 131189 | solution.py:220
  196.7 0.6 fusion.29
  197.3 1.4 bitcast_dynamic-update-slice_fusion.2
  198.6 0.6 fusion.29
  199.2 1.4 bitcast_dynamic-update-slice_fusion.2
  200.6 19.7 %custom-call.15 = f32[2,128,128]{1,2,0:T(8,128)S(1)} custom-call(f32[2,128,128]{2,1,0:T(8,128)S(1)} %get-tuple-element.9), custom_call_target="InvertDiagBlocksLowerTriangular" | custom-call | tf_op jit(solution)/shard_map/triangular_solve | solution.py:220
  220.3 0.3 fusion.3
  220.6 0.3 convolution_subtract_fusion
  220.8 0.3 fusion.8
  221.1 0.0 copy-done
  221.2 2.2 convolution_multiply_fusion
  (17 shorter events, 0.3 us)
Async XLA Ops:
  7.2 75.1 %all-gather.2.cloned.1.call-start = ((), (), s32[]{:S(2)}) async-start(), calls=%async_computation | async-start | bytes 2621440 | tf_op jit(solution)/shard_map/all_gather | solution.py:215
  61.3 95.9 %all-reduce.3.cloned.1.call-start = ((), (), s32[]{:S(2)}) async-start(), calls=%async_computation.1 | async-start | bytes 524288 | tf_op jit(solution)/shard_map/psum | solution.py:217
  171.0 50.1 %copy-start = (bf16[256,4096]{1,0:T(8,128)(2,1)S(1)}, bf16[256,4096]{1,0:T(8,128)(2,1)}, u32[]{:S(2)}) copy-start(bf16[256,4096]{1,0:T(8,128)(2,1)} %all-gather.2.cloned.1.call-done) | copy-start | bytes 6291460
Sparse Core Ops, SparseCore 0:
  61.4 20.7 all-gather.1
  86.2 71.0 all-reduce.2

commit v2 on v1

--- a/solution.py
+++ b/solution.py
@@ -1,3 +1,4 @@
+import functools
 import math
 
 import jax
@@ -59,9 +60,34 @@
     ).astype(jnp.int32)
 
 
-def filter_kernel(rows, lb, sc, tab, sub, ons, blk, out, bm, x0, x1, x2, x3, s0, y1, y2, y3,
-                  snd0, snd1, snd2, snd3, bsem, xsem, csem, ssem, rsem):
+def flip(c, bit):
+    return c + bit - 2 * bit * lax.rem(c // bit, 2)
+
+
+def hops_of(parts):
+    hops, held, bit = [], [0], parts // 2
+    while bit:
+        hops += [(bit, m) for m in held]
+        held += [m + bit for m in held]
+        bit //= 2
+    return hops
+
+
+def slice_of(width, rows):
+    return max(8, width // rows)
+
+
+def filter_kernel(rows, parts, lb, sc, tab, sub, ons, blk, out, gram, bm, x0, x1, x2, x3, s0, y1, y2, y3,
+                  snd0, snd1, snd2, snd3, gp, gs, rb, bsem, xsem, csem, ssem, rsem,
+                  wss, wrs, pss, prs, ass, ars):
     me = lax.axis_index("row")
+    mc = lax.axis_index("col")
+    everyone = rows * parts
+    linear = me * parts + mc
+    width = out.shape[2]
+    hops = hops_of(parts)
+    rps = slice_of(width, rows)
+    reducers = width // rps
     shifts = shifts_of(rows)
     groups = len(shifts)
     pn, pp = 0, lb * sc
@@ -93,8 +119,11 @@
         load(c).start()
 
     barrier = pltpu.get_barrier_semaphore()
-    for d in shifts:
-        pl.semaphore_signal(barrier, inc=1, device_id={"row": lax.rem(me + d + rows, rows)},
+
+    @pl.loop(1, everyone)
+    def _(e):
+        to = lax.rem(linear + e, everyone)
+        pl.semaphore_signal(barrier, inc=1, device_id=(to // parts, lax.rem(to, parts)),
                             device_id_type=pl.DeviceIdType.MESH)
 
     def copy(k, g):
@@ -102,7 +131,7 @@
             src_ref=snds[k].at[pl.ds(g * HALO, HALO)],
             dst_ref=xs[k].at[pl.ds(lb + g * HALO, HALO)],
             send_sem=ssem.at[k, g], recv_sem=rsem.at[k, g],
-            device_id={"row": lax.rem(me - shifts[g] + rows, rows)},
+            device_id=(lax.rem(me - shifts[g] + rows, rows), mc),
             device_id_type=pl.DeviceIdType.MESH)
 
     def pack(k, g, source, base):
@@ -115,7 +144,7 @@
 
     for g in range(groups):
         pack(0, g, s0, pexn)
-    pl.semaphore_wait(barrier, groups)
+    pl.semaphore_wait(barrier, everyone - 1)
 
     @pl.loop(0, lb)
     def _(i):
@@ -137,6 +166,19 @@
             return filter_scale * total
         prev = x0[i].astype(f32) if k == 1 else (y1[i] if k == 2 else y2[own])
         return 2.0 * filter_scale * total - prev
+
+    def spread(h, c):
+        bit, m = hops[h]
+        piece = mc
+        for b in (m & (1 << t) for t in range(m.bit_length())):
+            if b:
+                piece = flip(piece, b)
+        part = out.at[piece, pl.ds(c * UNROLL, UNROLL)]
+        return pltpu.make_async_remote_copy(
+            src_ref=part, dst_ref=part, send_sem=wss.at[h, c], recv_sem=wrs.at[h, c],
+            device_id=(me, flip(mc, bit)), device_id_type=pl.DeviceIdType.MESH)
+
+    firsts = [h for h, (_, m) in enumerate(hops) if m == 0]
 
     for k in range(FILTER):
         for g in range(groups):
@@ -160,7 +202,12 @@
                     xs[k + 1][j] = low
                     ys[j] = value
                 else:
-                    out[j] = low
+                    out[mc, j] = low
+                if k == FILTER - 1 and u == 1:
+                    @pl.when(c > 0)
+                    def _():
+                        for h in firsts:
+                            spread(h, c - 1).start()
                 if k in (1, 2) and u == 1:
                     for g in range(groups):
                         @pl.when(c == g + 1)
@@ -176,56 +223,226 @@
     for k in range(FILTER):
         for g in range(groups):
             copy(k, g).wait_send()
+    for h in firsts:
+        spread(h, chunks - 1).start()
+
+    @pl.loop(0, chunks)
+    def _(c):
+        got = set()
+        for h, (bit, m) in enumerate(hops):
+            if m:
+                source = max(hh for hh in range(h) if hops[hh][0] + hops[hh][1] == m)
+                if source not in got:
+                    spread(source, c).wait_recv()
+                    got.add(source)
+                spread(h, c).start()
+    relayed = {max(hh for hh in range(h) if hops[hh][0] + hops[hh][1] == m)
+               for h, (_, m) in enumerate(hops) if m}
+
+    @pl.loop(0, chunks)
+    def _(c):
+        for h in range(len(hops)):
+            if h not in relayed:
+                spread(h, c).wait_recv()
+            spread(h, c).wait_send()
+
+    gp[...] = jnp.zeros_like(gp)
+
+    @pl.loop(0, lb // 8)
+    def _(c):
+        cat = [jnp.concatenate([out[q, c * 8 + u] for u in range(8)], axis=1)
+               for q in range(parts)]
+        left = jnp.concatenate([out[mc, c * 8 + u] for u in range(8)], axis=1)
+        gp[...] += lax.dot_general(left, jnp.concatenate(cat, axis=0), (((1,), (1,)), ((), ())),
+                                   preferred_element_type=f32)
+
+    def part_to(d):
+        to = lax.rem(me + d, rows)
+        lo = pl.multiple_of(to * rps, rps)
+        return to, pltpu.make_async_remote_copy(
+            src_ref=gp.at[pl.ds(lo, rps)], dst_ref=rb.at[d], send_sem=pss.at[d],
+            recv_sem=prs.at[d], device_id=(to, mc), device_id_type=pl.DeviceIdType.MESH)
+
+    def part_in(d):
+        return pltpu.make_async_remote_copy(
+            src_ref=gp.at[pl.ds(0, rps)], dst_ref=rb.at[d], send_sem=pss.at[d],
+            recv_sem=prs.at[d], device_id=(lax.rem(me + 1, rows), mc),
+            device_id_type=pl.DeviceIdType.MESH)
+
+    def only(cond, run):
+        if reducers == rows:
+            run()
+        else:
+            pl.when(cond)(run)
+
+    @pl.loop(1, rows)
+    def _(d):
+        to, c = part_to(d)
+        only(to < reducers, lambda: c.start())
+
+    def all_to(e, sender):
+        to = lax.rem(linear + e, everyone)
+        lo = pl.multiple_of((lax.rem(sender, parts) * reducers + sender // parts) * rps, rps)
+        return pltpu.make_async_remote_copy(
+            src_ref=gs, dst_ref=gram.at[pl.ds(lo, rps)], send_sem=ass.at[e],
+            recv_sem=ars.at[e], device_id=(to // parts, lax.rem(to, parts)),
+            device_id_type=pl.DeviceIdType.MESH)
+
+    def reduce():
+        lo = pl.multiple_of(me * rps, rps)
+        total = gp[pl.ds(lo, rps)]
+        for d in range(1, rows):
+            part_in(d).wait_recv()
+            total = total + rb[d]
+        gs[...] = total
+        gram[pl.ds(pl.multiple_of((mc * reducers + me) * rps, rps), rps)] = total
+
+        @pl.loop(1, everyone)
+        def _(e):
+            all_to(e, linear).start()
+
+    only(me < reducers, reduce)
+
+    @pl.loop(1, rows)
+    def _(d):
+        to, c = part_to(d)
+        only(to < reducers, lambda: c.wait_send())
+
+    @pl.loop(1, everyone)
+    def _(e):
+        sender = lax.rem(linear - e + everyone, everyone)
+        only(me < reducers, lambda: all_to(e, linear).wait_send())
+        only(sender // parts < reducers, lambda: all_to(e, sender).wait_recv())
 
 
 def filtered(subspace, onsite, blocks, cols):
-    rows = lax.axis_size("row")
+    rows, parts = lax.axis_size("row"), lax.axis_size("col")
     me = lax.axis_index("row")
+    everyone, hops = rows * parts, len(hops_of(parts))
     width = subspace.shape[0]
     sc, lb, bs, _ = blocks.shape
     groups = len(shifts_of(rows))
     tab = index_tables(cols, rows, me, lb)
     ext = lb + groups * HALO
     vm, dma = pltpu.VMEM, pltpu.SemaphoreType.DMA
-    import functools
+    full = parts * width
+    rps = slice_of(width, rows)
     return pl.pallas_call(
-        functools.partial(filter_kernel, rows, lb, sc),
-        out_shape=jax.ShapeDtypeStruct((lb, width, bs), bf16),
+        functools.partial(filter_kernel, rows, parts, lb, sc),
+        out_shape=(jax.ShapeDtypeStruct((parts, lb, width, bs), bf16),
+                   jax.ShapeDtypeStruct((full, full), f32)),
         in_specs=[pl.BlockSpec(memory_space=pltpu.SMEM), pl.BlockSpec(memory_space=pl.ANY),
                   pl.BlockSpec(memory_space=pltpu.VMEM), pl.BlockSpec(memory_space=pl.ANY)],
-        out_specs=pl.BlockSpec(memory_space=pltpu.VMEM),
+        out_specs=[pl.BlockSpec(memory_space=pltpu.VMEM)] * 2,
         scratch_shapes=[vm((sc, lb, bs, bs), bf16)]
         + [vm((ext, width, bs), bf16)] * 4
         + [vm((lb, width, bs), bf16)]
         + [vm((lb, width, bs), f32)] * 3
         + [vm((groups * HALO, width, bs), bf16)] * 4
-        + [dma((lb // UNROLL,)), dma((lb,)), dma((lb,)), dma((FILTER, groups)), dma((FILTER, groups))],
+        + [vm((width, full), f32), vm((rps, full), f32), vm((rows, rps, full), f32)]
+        + [dma((lb // UNROLL,)), dma((lb,)), dma((lb,)), dma((FILTER, groups)), dma((FILTER, groups)),
+           dma((hops, lb // UNROLL)), dma((hops, lb // UNROLL)), dma((rows,)), dma((rows,)),
+           dma((everyone,)), dma((everyone,))],
         compiler_params=pltpu.CompilerParams(
             collective_id=0, has_side_effects=True, vmem_limit_bytes=56 * 1024 * 1024),
         name="filter",
     )(tab, subspace, onsite.reshape(lb, 1, bs), blocks)
 
 
+def eliminate(src, up, low):
+    n = src.shape[0]
+    tiles = n // 8
+    a = [src[8 * t:8 * t + 8, :] for t in range(tiles)]
+    sub = lax.broadcasted_iota(jnp.int32, (8, n), 0)
+    lane = lax.broadcasted_iota(jnp.int32, (8, n), 1)
+    b = [jnp.where(lane == sub + 8 * t, 1.0, 0.0).astype(f32) for t in range(tiles)]
+
+    def row(v, q):
+        return jnp.broadcast_to(v[q:q + 1, :], (8, n))
+
+    for p in range(tiles):
+        cols = {t: [jnp.broadcast_to(a[t][:, 8 * p + q:8 * p + q + 1], (8, n)) for q in range(8)]
+                for t in range(p, tiles)}
+        pivots = jnp.ones((8, n), f32)
+        for q in range(8):
+            pivot = row(cols[p][q], q)
+            pivots = jnp.where(sub == q, pivot, pivots)
+            inverse = 1.0 / pivot
+            right = [row(cols[p][k], q) for k in range(8)]
+            arow, brow = row(a[p], q), row(b[p], q)
+            for t in range(p, tiles):
+                m = cols[t][q] * inverse
+                if t == p:
+                    m = jnp.where(sub > q, m, 0.0)
+                for k in range(q + 1, 8):
+                    cols[t][k] = cols[t][k] - m * right[k]
+                a[t] = a[t] - m * arow
+                b[t] = b[t] - m * brow
+        scale = lax.rsqrt(pivots)
+        up[8 * p:8 * p + 8, :] = jnp.where(lane >= sub + 8 * p, a[p] * scale, 0.0)
+        low[8 * p:8 * p + 8, :] = b[p] * scale
+
+
+def finish_kernel(root, col, whole, gram, basis, factor, work, up, low, inv):
+    parts, lb, width, bs = whole.shape
+    full = gram.shape[0]
+    half = full // 2
+    exact = functools.partial(lax.dot_general, precision=lax.Precision.HIGHEST,
+                              preferred_element_type=f32)
+    nn, nt, tn = ((((1,), (0,)), ((), ())), (((1,), (1,)), ((), ())), (((0,), (0,)), ((), ())))
+    work[...] = gram[:half, :half]
+    factor[half:, :half] = jnp.zeros((half, half), f32)
+    inv[:half, half:] = jnp.zeros((half, half), f32)
+
+    @pl.loop(0, 2)
+    def _(i):
+        eliminate(work, up.at[i], low.at[i])
+
+        @pl.when(i == 0)
+        def _():
+            across = exact(low[0], gram[:half, half:], nn)
+            factor[:half, half:] = across * (1.0 / root)
+            work[...] = gram[half:, half:] - exact(across, across, tn)
+
+    across = factor[:half, half:] * root
+    inv[:half, :half] = low[0]
+    inv[half:, half:] = low[1]
+    inv[half:, :half] = -exact(low[1], exact(across, low[0], tn), nn)
+    factor[:half, :half] = up[0] * (1.0 / root)
+    factor[half:, half:] = up[1] * (1.0 / root)
+
+    mine = inv[pl.ds(pl.multiple_of(col[0] * width, width), width), :] * root
+    high = mine.astype(bf16)
+    rest = mine - high.astype(f32)
+    mid = rest.astype(bf16)
+    last = (rest - mid.astype(f32)).astype(bf16)
+    left = jnp.concatenate([high, mid, last], axis=0)
+
+    for k in range(lb):
+        right = jnp.concatenate([whole[q, k] for q in range(parts)], axis=0)
+        r = jnp.dot(left, right, preferred_element_type=f32)
+        basis[:, k * bs:(k + 1) * bs] = r[:width] + (r[width:2 * width] + r[2 * width:])
+
+
 def body(subspace, onsite, blocks, cols):
     row_count = lax.axis_size("row")
     part_width, local_rows = subspace.shape
-    final = filtered(subspace, onsite, blocks, cols)
-    final = jnp.transpose(final, (1, 0, 2)).reshape(part_width, local_rows)
-    S = part_width * lax.axis_size("col")
-    whole = lax.all_gather(final, "col", axis=0, tiled=True)
-    gram_local = jnp.einsum("ar,br->ab", whole, whole, preferred_element_type=jnp.float32)
-    gram = lax.psum(gram_local, "row")
-    lower = jnp.linalg.cholesky(gram)
-    total_rows = row_count * local_rows
-    inverse = lax.linalg.triangular_solve(
-        lower, jnp.eye(S, dtype=jnp.float32), left_side=True, lower=True
-    )
-    own_part = lax.dynamic_slice_in_dim(inverse, lax.axis_index("col") * part_width, part_width, 0)
-    basis = math.sqrt(total_rows) * jnp.dot(
-        own_part, whole.astype(jnp.float32), precision=lax.Precision.HIGHEST
-    )
-    factor = lower.T / math.sqrt(total_rows)
-    return (basis, factor)
+    whole, gram = filtered(subspace, onsite, blocks, cols)
+    full = gram.shape[0]
+    half = full // 2
+    root = math.sqrt(row_count * local_rows)
+    vm = pltpu.VMEM
+    return pl.pallas_call(
+        functools.partial(finish_kernel, root),
+        out_shape=(jax.ShapeDtypeStruct((part_width, local_rows), f32),
+                   jax.ShapeDtypeStruct((full, full), f32)),
+        in_specs=[pl.BlockSpec(memory_space=pltpu.SMEM)] + [pl.BlockSpec(memory_space=vm)] * 2,
+        out_specs=[pl.BlockSpec(memory_space=vm)] * 2,
+        scratch_shapes=[vm((half, half), f32), vm((2, half, half), f32), vm((2, half, half), f32),
+                        vm((full, full), f32)],
+        compiler_params=pltpu.CompilerParams(vmem_limit_bytes=32 * 1024 * 1024),
+        name="finish",
+    )(lax.axis_index("col").astype(jnp.int32).reshape(1), whole, gram)
 
 
 def solution(mesh):

time: 231 us -> 91.4 us (0.40)
  waiting for transfers between devices: 91.9 us -> 0 us
  other arithmetic: 56.6 us -> 1.26 us
  Pallas kernels: 48.1 us -> 83.7 us
  between operations: 15.6 us -> 0.75 us
  matrix products: 7.17 us -> 0 us
  local copies, waits for them, and re-layouts: 10.5 us -> 5.24 us
    psum x1 -> x0, waiting for transfers between devices: 71.2 us -> none  [body(): gram = lax.psum(gram_local, 'row')]
    another operation x9 -> x0, other arithmetic: 54.3 us -> none  [the longest x7 34.6 us: body(): lower = jnp.linalg.cholesky(gram)]
    pallas_call x1 -> x2, Pallas kernels: 48.1 us -> 83.7 us  [the longest x1 72.8 us: filtered(): pl.pallas_call(functools.partial(filter_kernel, rows, parts, lb, sc), out...]
    all_gather x1 -> x0, waiting for transfers between devices: 20.7 us -> none  [body(): whole = lax.all_gather(final, 'col', axis=0, tiled=True)]
    dot_general x2 -> x0, matrix products: 5.86 us -> none  [the longest x1 3.67 us: body(): jnp.einsum('ar,br->ab', whole, whole, preferred_element_type=jnp.float32)]
    another operation x9 -> x0, local copies, waits for them, and re-layouts: 3.99 us -> none
  transfers between devices with their start and end apart: 2 -> 0, of which waited for: 2 -> 0; matrix products, arithmetic and copies ran while one was open for 0% -> 0% of each run, Pallas kernels for 0% -> 0%
where the time goes in v2:
time: 91.4 us; the launch traced here: 91 us
  Pallas kernels  83.7 us (92%)
  local copies, waits for them, and re-layouts  5.24 us (6%)
  other arithmetic  1.26 us (1%)
    pallas_call x1, Pallas kernels, filtered(): pl.pallas_call(functools.partial(filter_kernel, rows, parts, lb, sc), out...  72.8 us
    pallas_call x1, Pallas kernels, body(): pl.pallas_call(functools.partial(finish_kernel, root), out_shape=(jax.Sha...  11 us
    unnamed x4, local copies, waits for them, and re-layouts  2.53 us

profile of v2, /device:TPU:0, one launch (start us, length us, event | category | flops | bytes accessed | tf_op | source)
XLA Modules:
  0.0 91.0 jit_solution(2352719224132726361)
XLA Ops:
  0.7 0.1 add_multiply_fusion
  0.8 0.9 %constant_dynamic-slice_fusion.4 = (s32[32,20]{0,1:T(8,128)S(1)}, s32[32,20]{0,1:T(8,128)S(1)}, s32[32,20]{0,1:T(8,128)S(1)}, s32[32,20]{0,1:T(8,128)S(1)}, s32[32,20]{0,1:T(8,128)S(1)}) fusion(s32[256,20]{0,1:T(8,128)} %param.7, s32[]{:T(128)S(6)} %select_n.45, s32[]{:T(128)S(6)} %select_n.47, s32[]{:T(128)S(6)} %select_n.46, s32[]{:T(128)S(6)} %select_n.49, ...), kind=kLoop, calls=%fused_computation.28 | loop fusion | bytes 25620 | tf_op jit(solution)/shard_map/dynamic_slice | solution.py:27
  1.7 0.1 copy.11
  1.8 0.1 reshape.115
  1.9 0.1 copy.13
  1.9 0.1 stack_reshape.13
  2.1 0.1 copy.12
  2.1 0.1 stack_reshape.12
  2.3 0.1 copy.15
  2.3 0.1 stack_reshape.15
  2.4 0.1 copy.14
  2.5 0.1 stack_reshape.14
  2.6 0.1 add_subtract_fusion
  2.7 0.2 fusion
  3.0 0.1 convert_reduce_fusion
  3.1 0.1 fusion.4
  3.2 0.1 select_reduce_fusion
  3.3 0.1 convert_reduce_fusion.1
  3.4 0.1 select_reduce_fusion.2
  3.5 0.2 select_reduce_fusion.3
  3.7 0.1 reshape.117
  3.8 0.1 reshape.116
  3.9 0.1 select_reduce_fusion.1
  4.0 0.7 concatenate.11.tab
  4.7 72.8 %filter.1 = (bf16[4,32,64,128]{3,2,1,0:T(8,128)(2,1)}, f32[256,256]{1,0:T(8,128)}) custom-call(s32[1376]{0:T(1024)} %concatenate.11.tab, bf16[64,4096]{1,0:T(8,128)(2,1)} %sub.54, f32[32,1,128]{2,1,0:T(1,128)} %bitcast.6, bf16[20,32,128,128]{3,2,1,0:T(8,128)(2,1)} %blk.1), custom_call_target="tpu_custom_call" | custom-call | tf_op jit(solution)/shard_map/filter/pallas_call | solution.py:330
  77.5 0.0 copy-start
  77.5 1.6 %copy-done = bf16[4,32,64,128]{3,2,1,0:T(8,128)(2,1)S(1)} copy-done((bf16[4,32,64,128]{3,2,1,0:T(8,128)(2,1)S(1)}, bf16[4,32,64,128]{3,2,1,0:T(8,128)(2,1)}, u32[]{:S(2)}) %copy-start) | copy-done | bytes 2097176
  79.1 0.0 copy-start.1
  79.1 0.9 %copy-done.1 = f32[256,256]{1,0:T(8,128)S(1)} copy-done((f32[256,256]{1,0:T(8,128)S(1)}, f32[256,256]{1,0:T(8,128)}, u32[]{:S(2)}) %copy-start.1) | copy-done | bytes 262168
  80.0 11.0 %finish.1 = (f32[64,4096]{1,0:T(8,128)}, f32[256,256]{1,0:T(8,128)}) custom-call(s32[1]{0:T(128)} %bitcast.col, bf16[4,32,64,128]{3,2,1,0:T(8,128)(2,1)S(1)} %copy-done, f32[256,256]{1,0:T(8,128)S(1)} %copy-done.1), custom_call_target="tpu_custom_call" | custom-call | tf_op jit(solution)/shard_map/finish/pallas_call | solution.py:435
  (7 shorter events, 0.1 us)
Async XLA Ops:
  77.5 1.6 %copy-start = (bf16[4,32,64,128]{3,2,1,0:T(8,128)(2,1)S(1)}, bf16[4,32,64,128]{3,2,1,0:T(8,128)(2,1)}, u32[]{:S(2)}) copy-start(bf16[4,32,64,128]{3,2,1,0:T(8,128)(2,1)} %get-tuple-element.4.whole) | copy-start | bytes 6291460
  79.1 0.9 %copy-start.1 = (f32[256,256]{1,0:T(8,128)S(1)}, f32[256,256]{1,0:T(8,128)}, u32[]{:S(2)}) copy-start(f32[256,256]{1,0:T(8,128)} %get-tuple-element.5.gram) | copy-start | bytes 786436

commit v3 on v2

--- a/solution.py
+++ b/solution.py
@@ -11,6 +11,7 @@
 HALO = 4
 FILTER = 4
 UNROLL = 4
+HALVES = 2
 filter_scale = 0.4
 f32 = jnp.float32
 bf16 = jnp.bfloat16
@@ -77,14 +78,21 @@
     return max(8, width // rows)
 
 
-def filter_kernel(rows, parts, lb, sc, tab, sub, ons, blk, out, gram, bm, x0, x1, x2, x3, s0, y1, y2, y3,
-                  snd0, snd1, snd2, snd3, gp, gs, rb, bsem, xsem, csem, ssem, rsem,
-                  wss, wrs, pss, prs, ass, ars):
+def filter_kernel(rows, parts, lb, sc, tab, sub, ons, blk, out, gram, bm, *refs):
+    refs = list(refs)
+    take = lambda n: [refs.pop(0) for _ in range(n)]
+    halves = range(HALVES)
+    xs = [take(HALVES) for _ in range(FILTER)]
+    snds = [take(HALVES) for _ in range(FILTER)]
+    ys = [take(HALVES) for _ in range(FILTER - 1)]
+    s0 = take(HALVES)
+    gp, gs, rb, bsem, xsem, csem, ssem, rsem, wss, wrs, pss, prs, ass, ars = refs
     me = lax.axis_index("row")
     mc = lax.axis_index("col")
     everyone = rows * parts
     linear = me * parts + mc
-    width = out.shape[2]
+    hw = out.shape[2]
+    width = hw * HALVES
     hops = hops_of(parts)
     rps = slice_of(width, rows)
     reducers = width // rps
@@ -95,7 +103,6 @@
     pinv = pperm + lb
     pexn = pinv + lb
     pexp = pexn + groups * HALO
-    xs, snds = (x0, x1, x2, x3), (snd0, snd1, snd2, snd3)
     bs = blk.shape[-1]
     chunks = lb // UNROLL
 
@@ -103,16 +110,17 @@
         part = pl.ds(c * UNROLL, UNROLL)
         return pltpu.make_async_copy(blk.at[:, part], bm.at[:, part], bsem.at[c])
 
-    def first(i):
-        cut = pl.ds(pl.multiple_of(i * bs, bs), bs)
-        return (pltpu.make_async_copy(sub.at[:, cut], x0.at[i], xsem.at[i]),
-                pltpu.make_async_copy(sub.at[:, cut], s0.at[i], csem.at[i]))
-
-    @pl.loop(0, lb)
-    def _(i):
-        a, b = first(i)
-        b.start()
-        a.start()
+    def first(i, h):
+        cut = sub.at[pl.ds(h * hw, hw), pl.ds(pl.multiple_of(i * bs, bs), bs)]
+        return (pltpu.make_async_copy(cut, xs[0][h].at[i], xsem.at[h, i]),
+                pltpu.make_async_copy(cut, s0[h].at[i], csem.at[h, i]))
+
+    for h in halves:
+        @pl.loop(0, lb)
+        def _(i):
+            a, b = first(i, h)
+            b.start()
+            a.start()
 
     @pl.loop(0, chunks)
     def _(c):
@@ -126,133 +134,134 @@
         pl.semaphore_signal(barrier, inc=1, device_id=(to // parts, lax.rem(to, parts)),
                             device_id_type=pl.DeviceIdType.MESH)
 
-    def copy(k, g):
+    def copy(k, h, g):
         return pltpu.make_async_remote_copy(
-            src_ref=snds[k].at[pl.ds(g * HALO, HALO)],
-            dst_ref=xs[k].at[pl.ds(lb + g * HALO, HALO)],
-            send_sem=ssem.at[k, g], recv_sem=rsem.at[k, g],
+            src_ref=snds[k][h].at[pl.ds(g * HALO, HALO)],
+            dst_ref=xs[k][h].at[pl.ds(lb + g * HALO, HALO)],
+            send_sem=ssem.at[k, h, g], recv_sem=rsem.at[k, h, g],
             device_id=(lax.rem(me - shifts[g] + rows, rows), mc),
             device_id_type=pl.DeviceIdType.MESH)
 
-    def pack(k, g, source, base):
+    def pack(k, h, g, source, base):
         for m in range(HALO):
-            snds[k][g * HALO + m] = source[tab[base + g * HALO + m]].astype(bf16)
-
-    @pl.loop(0, lb)
-    def _(i):
-        first(i)[1].wait()
-
-    for g in range(groups):
-        pack(0, g, s0, pexn)
-    pl.semaphore_wait(barrier, everyone - 1)
-
-    @pl.loop(0, lb)
-    def _(i):
-        first(i)[0].wait()
-
-    for g in range(groups):
-        copy(0, g).start()
-
-    def product(k, j):
-        i = tab[pperm + j] if k in (1, 2) else j
-        own = {0: j, 1: i, 2: j, 3: tab[pinv + j]}[k]
-        base = pn if k < 2 else pp
-        x = xs[k]
+            snds[k][h][g * HALO + m] = source[tab[base + g * HALO + m]].astype(bf16)
+
+    for h in halves:
+        @pl.loop(0, lb)
+        def _(i):
+            first(i, h)[1].wait()
+
+        for g in range(groups):
+            pack(0, h, g, s0[h], pexn)
+        if h == 0:
+            pl.semaphore_wait(barrier, everyone - 1)
+        for g in range(groups):
+            copy(0, h, g).start()
+
+    for h in halves:
+        @pl.loop(0, lb)
+        def _(i):
+            first(i, h)[0].wait()
+
+    def product(k, h, j):
+        i = j if k == FILTER - 1 else tab[pperm + j]
+        own = tab[pinv + j] if k == FILTER - 1 else (i if k == 0 else j)
+        base = pn if k == 0 else pp
+        x = xs[k][h]
         left = jnp.concatenate([x[tab[base + i * sc + s]] for s in range(sc)], axis=1)
         right = jnp.concatenate([bm[s, i] for s in range(sc)], axis=0)
         acc = jnp.dot(left, right, preferred_element_type=f32)
         total = acc + ons[i] * x[own].astype(f32)
         if k == 0:
             return filter_scale * total
-        prev = x0[i].astype(f32) if k == 1 else (y1[i] if k == 2 else y2[own])
+        prev = xs[0][h][i].astype(f32) if k == 1 else ys[k - 2][h][own]
         return 2.0 * filter_scale * total - prev
 
-    def spread(h, c):
-        bit, m = hops[h]
+    def spread(n, h, c):
+        bit, m = hops[n]
         piece = mc
         for b in (m & (1 << t) for t in range(m.bit_length())):
             if b:
                 piece = flip(piece, b)
-        part = out.at[piece, pl.ds(c * UNROLL, UNROLL)]
+        part = out.at[piece * HALVES + h, pl.ds(c * UNROLL, UNROLL)]
         return pltpu.make_async_remote_copy(
-            src_ref=part, dst_ref=part, send_sem=wss.at[h, c], recv_sem=wrs.at[h, c],
+            src_ref=part, dst_ref=part, send_sem=wss.at[n, h, c], recv_sem=wrs.at[n, h, c],
             device_id=(me, flip(mc, bit)), device_id_type=pl.DeviceIdType.MESH)
 
-    firsts = [h for h, (_, m) in enumerate(hops) if m == 0]
+    firsts = [n for n, (_, m) in enumerate(hops) if m == 0]
+
+    @pl.loop(0, chunks)
+    def _(c):
+        load(c).wait()
 
     for k in range(FILTER):
-        for g in range(groups):
-            copy(k, g).wait_recv()
-        ys = (y1, y2, y3, None)[k]
-
-        @pl.loop(0, chunks)
-        def _(c):
-            if k == 0:
-                load(c).wait()
-            if k in (1, 2):
-                for g in range(groups):
-                    @pl.when(c == g + 1)
-                    def _():
-                        pack(k + 1, g, ys, pexp)
-            for u in range(UNROLL):
-                j = c * UNROLL + u
-                value = product(k, j)
-                low = value.astype(bf16)
+        for h in halves:
+            for g in range(groups):
+                copy(k, h, g).wait_recv()
+
+            @pl.loop(0, chunks)
+            def _(c):
                 if k < FILTER - 1:
-                    xs[k + 1][j] = low
-                    ys[j] = value
-                else:
-                    out[mc, j] = low
-                if k == FILTER - 1 and u == 1:
-                    @pl.when(c > 0)
-                    def _():
-                        for h in firsts:
-                            spread(h, c - 1).start()
-                if k in (1, 2) and u == 1:
                     for g in range(groups):
                         @pl.when(c == g + 1)
                         def _():
-                            copy(k + 1, g).start()
-
-        if k == 0:
+                            pack(k + 1, h, g, ys[k][h], pexp)
+                for u in range(UNROLL):
+                    j = c * UNROLL + u
+                    value = product(k, h, j)
+                    low = value.astype(bf16)
+                    if k < FILTER - 1:
+                        xs[k + 1][h][j] = low
+                        ys[k][h][j] = value
+                        if u == 1:
+                            for g in range(groups):
+                                @pl.when(c == g + 1)
+                                def _():
+                                    copy(k + 1, h, g).start()
+                    else:
+                        out[mc * HALVES + h, j] = low
+                        if u == 1:
+                            @pl.when(c > 0)
+                            def _():
+                                for n in firsts:
+                                    spread(n, h, c - 1).start()
+            if k == FILTER - 1:
+                for n in firsts:
+                    spread(n, h, chunks - 1).start()
+
+    for k in range(FILTER):
+        for h in halves:
             for g in range(groups):
-                pack(1, g, ys, pexn)
-            for g in range(groups):
-                copy(1, g).start()
-
-    for k in range(FILTER):
-        for g in range(groups):
-            copy(k, g).wait_send()
-    for h in firsts:
-        spread(h, chunks - 1).start()
-
-    @pl.loop(0, chunks)
-    def _(c):
-        got = set()
-        for h, (bit, m) in enumerate(hops):
-            if m:
-                source = max(hh for hh in range(h) if hops[hh][0] + hops[hh][1] == m)
-                if source not in got:
-                    spread(source, c).wait_recv()
-                    got.add(source)
-                spread(h, c).start()
-    relayed = {max(hh for hh in range(h) if hops[hh][0] + hops[hh][1] == m)
-               for h, (_, m) in enumerate(hops) if m}
-
-    @pl.loop(0, chunks)
-    def _(c):
-        for h in range(len(hops)):
-            if h not in relayed:
-                spread(h, c).wait_recv()
-            spread(h, c).wait_send()
+                copy(k, h, g).wait_send()
+
+    needs = {n: max(q for q in range(n) if sum(hops[q]) == m)
+             for n, (_, m) in enumerate(hops) if m}
+    for h in halves:
+        @pl.loop(0, chunks)
+        def _(c):
+            got = set()
+            for n in needs:
+                if needs[n] not in got:
+                    spread(needs[n], h, c).wait_recv()
+                    got.add(needs[n])
+                spread(n, h, c).start()
+    for h in halves:
+        @pl.loop(0, chunks)
+        def _(c):
+            for n in range(len(hops)):
+                if n not in needs.values():
+                    spread(n, h, c).wait_recv()
+                spread(n, h, c).wait_send()
 
     gp[...] = jnp.zeros_like(gp)
 
     @pl.loop(0, lb // 8)
     def _(c):
         cat = [jnp.concatenate([out[q, c * 8 + u] for u in range(8)], axis=1)
-               for q in range(parts)]
-        left = jnp.concatenate([out[mc, c * 8 + u] for u in range(8)], axis=1)
+               for q in range(parts * HALVES)]
+        left = jnp.concatenate([jnp.concatenate([out[mc * HALVES + h, c * 8 + u]
+                                                 for u in range(8)], axis=1)
+                                for h in halves], axis=0)
         gp[...] += lax.dot_general(left, jnp.concatenate(cat, axis=0), (((1,), (1,)), ((), ())),
                                    preferred_element_type=f32)
 
@@ -325,24 +334,25 @@
     tab = index_tables(cols, rows, me, lb)
     ext = lb + groups * HALO
     vm, dma = pltpu.VMEM, pltpu.SemaphoreType.DMA
-    full = parts * width
+    full, hw = parts * width, width // HALVES
     rps = slice_of(width, rows)
     return pl.pallas_call(
         functools.partial(filter_kernel, rows, parts, lb, sc),
-        out_shape=(jax.ShapeDtypeStruct((parts, lb, width, bs), bf16),
+        out_shape=(jax.ShapeDtypeStruct((parts * HALVES, lb, hw, bs), bf16),
                    jax.ShapeDtypeStruct((full, full), f32)),
         in_specs=[pl.BlockSpec(memory_space=pltpu.SMEM), pl.BlockSpec(memory_space=pl.ANY),
                   pl.BlockSpec(memory_space=pltpu.VMEM), pl.BlockSpec(memory_space=pl.ANY)],
         out_specs=[pl.BlockSpec(memory_space=pltpu.VMEM)] * 2,
         scratch_shapes=[vm((sc, lb, bs, bs), bf16)]
-        + [vm((ext, width, bs), bf16)] * 4
-        + [vm((lb, width, bs), bf16)]
-        + [vm((lb, width, bs), f32)] * 3
-        + [vm((groups * HALO, width, bs), bf16)] * 4
+        + [vm((ext, hw, bs), bf16)] * (FILTER * HALVES)
+        + [vm((groups * HALO, hw, bs), bf16)] * (FILTER * HALVES)
+        + [vm((lb, hw, bs), f32)] * ((FILTER - 1) * HALVES)
+        + [vm((lb, hw, bs), bf16)] * HALVES
         + [vm((width, full), f32), vm((rps, full), f32), vm((rows, rps, full), f32)]
-        + [dma((lb // UNROLL,)), dma((lb,)), dma((lb,)), dma((FILTER, groups)), dma((FILTER, groups)),
-           dma((hops, lb // UNROLL)), dma((hops, lb // UNROLL)), dma((rows,)), dma((rows,)),
-           dma((everyone,)), dma((everyone,))],
+        + [dma((lb // UNROLL,)), dma((HALVES, lb)), dma((HALVES, lb)),
+           dma((FILTER, HALVES, groups)), dma((FILTER, HALVES, groups)),
+           dma((hops, HALVES, lb // UNROLL)), dma((hops, HALVES, lb // UNROLL)),
+           dma((rows,)), dma((rows,)), dma((everyone,)), dma((everyone,))],
         compiler_params=pltpu.CompilerParams(
             collective_id=0, has_side_effects=True, vmem_limit_bytes=56 * 1024 * 1024),
         name="filter",
@@ -384,7 +394,8 @@
 
 
 def finish_kernel(root, col, whole, gram, basis, factor, work, up, low, inv):
-    parts, lb, width, bs = whole.shape
+    parts, lb, _, bs = whole.shape
+    width = basis.shape[0]
     full = gram.shape[0]
     half = full // 2
     exact = functools.partial(lax.dot_general, precision=lax.Precision.HIGHEST,

time: 91.4 us -> 99.2 us (1.085)
  Pallas kernels: 83.7 us -> 91.5 us
    pallas_call x1, Pallas kernels: 72.8 us -> 80.6 us  [filtered(): pl.pallas_call(functools.partial(filter_kernel, rows, parts, lb, sc), out...]
where the time goes in v3:
time: 99.2 us; the launch traced here: 98.8 us
  Pallas kernels  91.5 us (92%)
  local copies, waits for them, and re-layouts  5.24 us (5%)
  other arithmetic  1.26 us (1%)
    pallas_call x1, Pallas kernels, filtered(): pl.pallas_call(functools.partial(filter_kernel, rows, parts, lb, sc), out...  80.6 us
    pallas_call x1, Pallas kernels, body(): pl.pallas_call(functools.partial(finish_kernel, root), out_shape=(jax.Sha...  10.9 us
    unnamed x4, local copies, waits for them, and re-layouts  2.53 us

profile of v3, /device:TPU:0, one launch (start us, length us, event | category | flops | bytes accessed | tf_op | source)
XLA Modules:
  0.0 98.8 jit_solution(2981992552547733530)
XLA Ops:
  0.7 0.1 add_multiply_fusion
  0.8 0.9 constant_dynamic-slice_fusion.4
  1.7 0.1 copy.11
  1.8 0.1 reshape.115
  1.9 0.1 copy.13
  1.9 0.1 stack_reshape.13
  2.1 0.1 copy.12
  2.1 0.1 stack_reshape.12
  2.3 0.1 copy.15
  2.3 0.1 stack_reshape.15
  2.4 0.1 copy.14
  2.5 0.1 stack_reshape.14
  2.6 0.1 add_subtract_fusion
  2.7 0.2 fusion
  3.0 0.1 convert_reduce_fusion
  3.1 0.1 fusion.4
  3.2 0.1 select_reduce_fusion
  3.3 0.1 convert_reduce_fusion.1
  3.4 0.1 select_reduce_fusion.2
  3.5 0.2 select_reduce_fusion.3
  3.7 0.1 reshape.117
  3.8 0.1 reshape.116
  3.9 0.1 select_reduce_fusion.1
  4.0 0.7 concatenate.11.tab
  4.7 80.6 %filter.1 = (bf16[8,32,32,128]{3,2,1,0:T(8,128)(2,1)}, f32[256,256]{1,0:T(8,128)}) custom-call(s32[1376]{0:T(1024)} %concatenate.11.tab, bf16[64,4096]{1,0:T(8,128)(2,1)} %sub.54, f32[32,1,128]{2,1,0:T(1,128)} %bitcast.6, bf16[20,32,128,128]{3,2,1,0:T(8,128)(2,1)} %blk.1), custom_call_target="tpu_custom_call" | custom-call | tf_op jit(solution)/shard_map/filter/pallas_call | solution.py:339
  85.3 0.0 copy-start
  85.3 1.6 %copy-done = bf16[8,32,32,128]{3,2,1,0:T(8,128)(2,1)S(1)} copy-done((bf16[8,32,32,128]{3,2,1,0:T(8,128)(2,1)S(1)}, bf16[8,32,32,128]{3,2,1,0:T(8,128)(2,1)}, u32[]{:S(2)}) %copy-start) | copy-done | bytes 2097176
  86.9 0.0 copy-start.1
  86.9 0.9 copy-done.1
  87.8 10.9 %finish.1 = (f32[64,4096]{1,0:T(8,128)}, f32[256,256]{1,0:T(8,128)}) custom-call(s32[1]{0:T(128)} %bitcast.col, bf16[8,32,32,128]{3,2,1,0:T(8,128)(2,1)S(1)} %copy-done, f32[256,256]{1,0:T(8,128)S(1)} %copy-done.1), custom_call_target="tpu_custom_call" | custom-call | tf_op jit(solution)/shard_map/finish/pallas_call | solution.py:446
  (7 shorter events, 0.1 us)
Async XLA Ops:
  85.3 1.6 %copy-start = (bf16[8,32,32,128]{3,2,1,0:T(8,128)(2,1)S(1)}, bf16[8,32,32,128]{3,2,1,0:T(8,128)(2,1)}, u32[]{:S(2)}) copy-start(bf16[8,32,32,128]{3,2,1,0:T(8,128)(2,1)} %get-tuple-element.4.whole) | copy-start | bytes 6291460
  86.9 0.9 copy-start.1

commit v4 on v3

--- a/solution.py
+++ b/solution.py
@@ -11,7 +11,7 @@
 HALO = 4
 FILTER = 4
 UNROLL = 4
-HALVES = 2
+HALVES = 1
 filter_scale = 0.4
 f32 = jnp.float32
 bf16 = jnp.bfloat16
@@ -393,7 +393,9 @@
         low[8 * p:8 * p + 8, :] = b[p] * scale
 
 
-def finish_kernel(root, col, whole, gram, basis, factor, work, up, low, inv):
+def finish_kernel(root, col, stored, gram, basis, factor, work, up, low, inv, whole, sem):
+    fetch = pltpu.make_async_copy(stored, whole, sem)
+    fetch.start()
     parts, lb, _, bs = whole.shape
     width = basis.shape[0]
     full = gram.shape[0]
@@ -429,6 +431,7 @@
     last = (rest - mid.astype(f32)).astype(bf16)
     left = jnp.concatenate([high, mid, last], axis=0)
 
+    fetch.wait()
     for k in range(lb):
         right = jnp.concatenate([whole[q, k] for q in range(parts)], axis=0)
         r = jnp.dot(left, right, preferred_element_type=f32)
@@ -447,10 +450,11 @@
         functools.partial(finish_kernel, root),
         out_shape=(jax.ShapeDtypeStruct((part_width, local_rows), f32),
                    jax.ShapeDtypeStruct((full, full), f32)),
-        in_specs=[pl.BlockSpec(memory_space=pltpu.SMEM)] + [pl.BlockSpec(memory_space=vm)] * 2,
+        in_specs=[pl.BlockSpec(memory_space=pltpu.SMEM), pl.BlockSpec(memory_space=pltpu.HBM),
+                  pl.BlockSpec(memory_space=vm)],
         out_specs=[pl.BlockSpec(memory_space=vm)] * 2,
         scratch_shapes=[vm((half, half), f32), vm((2, half, half), f32), vm((2, half, half), f32),
-                        vm((full, full), f32)],
+                        vm((full, full), f32), vm(whole.shape, bf16), pltpu.SemaphoreType.DMA],
         compiler_params=pltpu.CompilerParams(vmem_limit_bytes=32 * 1024 * 1024),
         name="finish",
     )(lax.axis_index("col").astype(jnp.int32).reshape(1), whole, gram)

time: 99.2 us -> 87.9 us (0.89)
  Pallas kernels: 91.5 us -> 80.4 us
    pallas_call x1, Pallas kernels: 80.6 us -> 69.3 us  [filtered(): pl.pallas_call(functools.partial(filter_kernel, rows, parts, lb, sc), out...]
where the time goes in v4:
time: 87.9 us; the launch traced here: 87.6 us
  Pallas kernels  80.4 us (91%)
  local copies, waits for them, and re-layouts  5.24 us (6%)
  other arithmetic  1.26 us (1%)
    pallas_call x1, Pallas kernels, filtered(): pl.pallas_call(functools.partial(filter_kernel, rows, parts, lb, sc), out...  69.3 us
    pallas_call x1, Pallas kernels, body(): pl.pallas_call(functools.partial(finish_kernel, root), out_shape=(jax.Sha...  11.1 us
    unnamed x4, local copies, waits for them, and re-layouts  2.53 us

profile of v4, /device:TPU:0, one launch (start us, length us, event | category | flops | bytes accessed | tf_op | source)
XLA Modules:
  0.0 87.6 jit_solution(3458299833406188684)
XLA Ops:
  0.7 0.1 add_multiply_fusion
  0.8 0.9 %constant_dynamic-slice_fusion.4 = (s32[32,20]{0,1:T(8,128)S(1)}, s32[32,20]{0,1:T(8,128)S(1)}, s32[32,20]{0,1:T(8,128)S(1)}, s32[32,20]{0,1:T(8,128)S(1)}, s32[32,20]{0,1:T(8,128)S(1)}) fusion(s32[256,20]{0,1:T(8,128)} %param.7, s32[]{:T(128)S(6)} %select_n.45, s32[]{:T(128)S(6)} %select_n.47, s32[]{:T(128)S(6)} %select_n.46, s32[]{:T(128)S(6)} %select_n.49, ...), kind=kLoop, calls=%fused_computation.28 | loop fusion | bytes 25620 | tf_op jit(solution)/shard_map/dynamic_slice | solution.py:28
  1.7 0.1 copy.11
  1.8 0.1 reshape.115
  1.9 0.1 copy.13
  1.9 0.1 stack_reshape.13
  2.1 0.1 copy.12
  2.1 0.1 stack_reshape.12
  2.3 0.1 copy.15
  2.3 0.1 stack_reshape.15
  2.4 0.1 copy.14
  2.5 0.1 stack_reshape.14
  2.6 0.1 add_subtract_fusion
  2.7 0.2 fusion
  3.0 0.1 convert_reduce_fusion
  3.1 0.1 fusion.4
  3.2 0.1 select_reduce_fusion
  3.3 0.1 convert_reduce_fusion.1
  3.4 0.1 select_reduce_fusion.2
  3.5 0.2 select_reduce_fusion.3
  3.7 0.1 reshape.117
  3.8 0.1 reshape.116
  3.9 0.1 select_reduce_fusion.1
  4.0 0.7 concatenate.11.tab
  4.7 69.3 %filter.1 = (bf16[4,32,64,128]{3,2,1,0:T(8,128)(2,1)}, f32[256,256]{1,0:T(8,128)}) custom-call(s32[1376]{0:T(1024)} %concatenate.11.tab, bf16[64,4096]{1,0:T(8,128)(2,1)} %sub.54, f32[32,1,128]{2,1,0:T(1,128)} %bitcast.6, bf16[20,32,128,128]{3,2,1,0:T(8,128)(2,1)} %blk.1), custom_call_target="tpu_custom_call" | custom-call | tf_op jit(solution)/shard_map/filter/pallas_call | solution.py:339
  74.0 0.0 copy-start
  74.0 1.6 %copy-done = bf16[4,32,64,128]{3,2,1,0:T(8,128)(2,1)S(1)} copy-done((bf16[4,32,64,128]{3,2,1,0:T(8,128)(2,1)S(1)}, bf16[4,32,64,128]{3,2,1,0:T(8,128)(2,1)}, u32[]{:S(2)}) %copy-start) | copy-done | bytes 2097176
  75.6 0.0 copy-start.1
  75.6 0.9 %copy-done.1 = f32[256,256]{1,0:T(8,128)S(1)} copy-done((f32[256,256]{1,0:T(8,128)S(1)}, f32[256,256]{1,0:T(8,128)}, u32[]{:S(2)}) %copy-start.1) | copy-done | bytes 262168
  76.5 11.1 %finish.1 = (f32[64,4096]{1,0:T(8,128)}, f32[256,256]{1,0:T(8,128)}) custom-call(s32[1]{0:T(128)} %bitcast.col, bf16[4,32,64,128]{3,2,1,0:T(8,128)(2,1)S(1)} %copy-done, f32[256,256]{1,0:T(8,128)S(1)} %copy-done.1), custom_call_target="tpu_custom_call" | custom-call | tf_op jit(solution)/shard_map/finish/pallas_call | solution.py:449
  (7 shorter events, 0.1 us)
Async XLA Ops:
  74.0 1.6 %copy-start = (bf16[4,32,64,128]{3,2,1,0:T(8,128)(2,1)S(1)}, bf16[4,32,64,128]{3,2,1,0:T(8,128)(2,1)}, u32[]{:S(2)}) copy-start(bf16[4,32,64,128]{3,2,1,0:T(8,128)(2,1)} %get-tuple-element.4.stored) | copy-start | bytes 6291460
  75.6 0.9 %copy-start.1 = (f32[256,256]{1,0:T(8,128)S(1)}, f32[256,256]{1,0:T(8,128)}, u32[]{:S(2)}) copy-start(f32[256,256]{1,0:T(8,128)} %get-tuple-element.5.gram) | copy-start | bytes 786436
